TPU v7x, 32 devices: a whole 2x2x4 slice. The times are simulated.
32 devices in a mesh: rad: 8 (over z, y), ell: 4 (over x, core).
Axes of the slice: x: 2, y: 2, z: 4, core: 2. Of those that a mesh axis runs over, the one named last changes fastest.
Arguments:
- field: bfloat16 [512, 128, 512], P('rad', 'ell'), may hold values from -6 to 6
- projection: bfloat16 [512, 128, 256], P('rad', 'ell'), may hold values from -0.375 to 0.375
- ell_ids: int32 [128], P('ell'), may hold values from 0 to 255, as said below
Outputs:
- share: float32 [128, 256], P('ell', 'rad')
- crest: float32 [128, 256], P('ell', 'rad')
Inputs may be any that keep to these rules, and one draw needn't show every extreme that they name: `ell_ids`: distinct and ascending.
All inputs are finite; a program needn't handle non-finite values.
Results may differ from a plain program's by a relative error of at most 0.0003.
Values may be sent and summed in bfloat16 or wider, within the bound.
A program may use at most 64 MiB of HBM per device.

v0:
```python
import jax
import jax.numpy as jnp
from jax import lax
from jax.sharding import PartitionSpec as P


def per_device(field, projection, ell_ids):
    exchanged = lax.all_to_all(field, "rad", split_axis=2, concat_axis=0, tiled=True)
    slot_share = exchanged.shape[2]
    coef = jnp.einsum(
        "rem,ren->emn",
        exchanged,
        lax.all_gather(projection, "rad", axis=0, tiled=True),
        preferred_element_type=jnp.float32,
    )
    slots = lax.axis_index("rad") * slot_share + jnp.arange(slot_share, dtype=jnp.int32)
    valid = (slots[None, :] < 2 * ell_ids[:, None] + 1).astype(jnp.float32)
    energy_part = jnp.sum(valid[:, :, None] * coef * coef, axis=1)
    peak_part = jnp.max(valid[:, :, None] * jnp.abs(coef), axis=1)
    energy_all, peak_all = (
        lax.all_to_all(energy_part[None], "rad", split_axis=2, concat_axis=0, tiled=True),
        lax.all_to_all(peak_part[None], "rad", split_axis=2, concat_axis=0, tiled=True),
    )
    energy = jnp.sum(energy_all, axis=0)
    peak = jnp.max(peak_all, axis=0)
    local_sum = jnp.sum(energy, axis=0)
    local_top = jnp.max(peak, axis=0)
    column = lax.psum(local_sum, "ell")
    top = lax.pmax(local_top, "ell")
    column = column + 1e-06
    top = top + 1e-06
    total_ells = ell_ids.shape[0] * lax.axis_size("ell")
    share = total_ells * energy / column[None, :]
    crest = peak / top[None, :]
    return (share, crest)


def solution(mesh):
    in_specs = (P("rad", "ell", None), P("rad", "ell", None), P("ell"))
    out_specs = (P("ell", "rad"), P("ell", "rad"))
    return jax.shard_map(
        per_device, mesh=mesh, in_specs=in_specs, out_specs=out_specs, check_vma=False
    )
```

profile of v0, /device:TPU:0, one launch (start us, length us, event | category | flops | bytes accessed | tf_op | source)
XLA Modules:
  0.0 218.3 jit_solution(14163633866488096663)
XLA Ops:
  7.2 2.9 %copy.19 = bf16[64,32,256]{2,0,1:T(8,128)(2,1)} copy(bf16[64,32,256]{2,1,0:T(8,128)(2,1)} %param.4) | data formatting | bytes 2097152 | tf_op args[1]
  10.2 7.8 %copy.17 = bf16[64,32,512]{0,1,2:T(8,128)(2,1)} copy(bf16[64,32,512]{2,1,0:T(8,128)(2,1)S(1)} %copy-done) | data formatting | bytes 4194304 | tf_op args[0]
  18.0 7.7 %reshape.45 = bf16[8,2,65536]{2,1,0:T(2,128)(2,1)} reshape(bf16[512,32,64]{2,1,0:T(8,128)(2,1)} %bitcast.22) | data formatting | bytes 4194304
  25.7 7.5 %all-to-all-start = ((bf16[8,2,65536]{2,1,0:T(2,128)(2,1)}), bf16[8,2,65536]{2,1,0:T(2,128)(2,1)S(1)}, u32[]{:S(2)}, u32[]{:S(2)}) async-start(bf16[8,2,65536]{2,1,0:T(2,128)(2,1)} %reshape.45), calls=%async_computation | async-start | bytes 4194304 | tf_op jit(solution)/shard_map/all_to_all | solution.py:8
  33.2 87.4 %all-to-all-done = bf16[8,2,65536]{2,1,0:T(2,128)(2,1)S(1)} async-done(((bf16[8,2,65536]{2,1,0:T(2,128)(2,1)}), bf16[8,2,65536]{2,1,0:T(2,128)(2,1)S(1)}, u32[]{:S(2)}, u32[]{:S(2)}) %all-to-all-start) | async-done | bytes 2097184 | tf_op jit(solution)/shard_map/all_to_all | solution.py:8
  120.7 5.0 %reshape.46 = bf16[512,32,64]{2,1,0:T(8,128)(2,1)} reshape(bf16[8,2,65536]{2,1,0:T(2,128)(2,1)S(1)} %all-to-all-done) | data formatting | bytes 4194304
  125.7 6.8 %copy.25 = bf16[64,32,8,64]{0,2,3,1:T(8,128)(2,1)} copy(bf16[64,32,8,64]{0,1,3,2:T(8,128)(2,1)} %bitcast.23) | data formatting | bytes 4194304 | tf_op jit(solution)/shard_map/all_to_all | solution.py:8
  132.5 5.4 %all_to_all.34 = bf16[512,32,64]{0,2,1:T(8,128)(2,1)S(1)} reshape(bf16[8,64,32,64]{1,0,3,2:T(8,128)(2,1)} %bitcast.24) | data formatting | bytes 4194304 | tf_op jit(solution)/shard_map/all_to_all | solution.py:8
  137.9 35.0 %all-gather.2.cloned.1.call-done = bf16[512,32,256]{2,0,1:T(8,128)(2,1)} async-done(((bf16[64,32,256]{2,0,1:T(8,128)(2,1)}), bf16[512,32,256]{2,0,1:T(8,128)(2,1)}) %all-gather.2.cloned.1.call-update) | async-done | bytes 8388624 | tf_op jit(solution)/shard_map/all_gather | solution.py:13
  172.9 4.9 %multiply_reduce_fusion = (f32[32,256]{1,0:T(8,128)S(1)}, f32[32,256]{1,0:T(8,128)S(1)}) fusion(f32[32,64]{1,0:T(8,128)S(1)} %compare_convert_fusion, bf16[512,32,64]{0,2,1:T(8,128)(2,1)S(1)} %all_to_all.34, bf16[512,32,256]{2,0,1:T(8,128)(2,1)} %all-gather.2.cloned.1.call-done), kind=kOutput, calls=%fused_computation.3 | convolution fusion | flops 540000256 | bytes 10559488 | tf_op jit(solution)/shard_map/rem,ren->emn/dot_general | solution.py:10
  178.4 1.0 reduce.18
  179.4 0.7 reshape.49
  180.1 3.3 %all-to-all-start.2 = ((f32[8,1,1024]{2,1,0:T(1,128)}), f32[8,1,1024]{2,1,0:T(1,128)S(1)}, u32[]{:S(2)}, u32[]{:S(2)}) async-start(f32[8,1,1024]{2,1,0:T(1,128)} %reshape.49), calls=%async_computation.2 | async-start | bytes 65536 | tf_op jit(solution)/shard_map/all_to_all | solution.py:22
  183.6 1.0 reduce.16
  184.6 0.7 reshape.47
  185.3 4.8 %all-to-all-done.2 = f32[8,1,1024]{2,1,0:T(1,128)S(1)} async-done(((f32[8,1,1024]{2,1,0:T(1,128)}), f32[8,1,1024]{2,1,0:T(1,128)S(1)}, u32[]{:S(2)}, u32[]{:S(2)}) %all-to-all-start.2) | async-done | bytes 32800 | tf_op jit(solution)/shard_map/all_to_all | solution.py:22
  190.1 3.3 %all-to-all-start.1 = ((f32[8,1,1024]{2,1,0:T(1,128)}), f32[8,1,1024]{2,1,0:T(1,128)S(1)}, u32[]{:S(2)}, u32[]{:S(2)}) async-start(f32[8,1,1024]{2,1,0:T(1,128)} %reshape.47), calls=%async_computation.1 | async-start | bytes 65536 | tf_op jit(solution)/shard_map/all_to_all | solution.py:21
  193.4 0.7 reduce.19
  194.4 1.0 bitcast_reduce_fusion
  195.6 6.0 %pmax.7 = f32[32]{0:T(128)S(1)} all-reduce(f32[32]{0:T(128)S(1)} %reduce_max.38), channel_id=1, replica_groups=mesh['rad'=8,'ell'=4] {'ell'}, use_global_device_ids=true, to_apply=%region_9.10 | all-reduce | flops 32 | bytes 256 | tf_op jit(solution)/shard_map/pmax | solution.py:29
  201.6 0.7 copy.23
  202.3 0.7 reduce.17
  203.2 1.0 bitcast_reduce_fusion.1
  204.4 6.3 %psum.7 = f32[32]{0:T(128)S(1)} all-reduce(f32[32]{0:T(128)S(1)} %reduce_sum.38), channel_id=1, replica_groups=mesh['rad'=8,'ell'=4] {'ell'}, use_global_device_ids=true, to_apply=%region_4.0 | all-reduce | flops 32 | bytes 256 | tf_op jit(solution)/shard_map/psum | solution.py:28
  (26 shorter events, 2.4 us)
Async XLA Ops:
  7.2 3.0 %copy-start = (bf16[64,32,512]{2,1,0:T(8,128)(2,1)S(1)}, bf16[64,32,512]{2,1,0:T(8,128)(2,1)}, u32[]{:S(2)}) copy-start(bf16[64,32,512]{2,1,0:T(8,128)(2,1)} %param.3) | copy-start | bytes 6291460
  7.2 165.7 %all-gather.2.cloned.1.call-start = ((), (), s32[]{:S(2)}) async-start(), calls=%async_computation.3 | async-start | bytes 9437184 | tf_op jit(solution)/shard_map/all_gather | solution.py:13
  25.7 7.5 %copy-start.1 = (s32[32]{0:T(128)S(1)}, s32[32]{0:T(128)}, u32[]{:S(2)}) copy-start(s32[32]{0:T(128)} %param.5) | copy-start | bytes 388
  25.7 95.0 %all-to-all-start = ((bf16[8,2,65536]{2,1,0:T(2,128)(2,1)}), bf16[8,2,65536]{2,1,0:T(2,128)(2,1)S(1)}, u32[]{:S(2)}, u32[]{:S(2)}) async-start(bf16[8,2,65536]{2,1,0:T(2,128)(2,1)} %reshape.45), calls=%async_computation | async-start | bytes 4194304 | tf_op jit(solution)/shard_map/all_to_all | solution.py:8
  180.1 10.0 %all-to-all-start.2 = ((f32[8,1,1024]{2,1,0:T(1,128)}), f32[8,1,1024]{2,1,0:T(1,128)S(1)}, u32[]{:S(2)}, u32[]{:S(2)}) async-start(f32[8,1,1024]{2,1,0:T(1,128)} %reshape.49), calls=%async_computation.2 | async-start | bytes 65536 | tf_op jit(solution)/shard_map/all_to_all | solution.py:22
  190.1 12.2 %all-to-all-start.1 = ((f32[8,1,1024]{2,1,0:T(1,128)}), f32[8,1,1024]{2,1,0:T(1,128)S(1)}, u32[]{:S(2)}, u32[]{:S(2)}) async-start(f32[8,1,1024]{2,1,0:T(1,128)} %reshape.47), calls=%async_computation.1 | async-start | bytes 65536 | tf_op jit(solution)/shard_map/all_to_all | solution.py:21
Sparse Core Ops, SparseCore 0:
  10.3 162.5 all-gather.1
where the time goes:
time: 219 us; the launch traced here: 218 us
  waiting for transfers between devices  127 us (58%)
  local copies, waits for them, and re-layouts  39.8 us (18%)
  starting transfers between devices  14.2 us (6%)
  between operations  14.2 us (6%)
  blocking collectives  12.3 us (6%)
  other arithmetic  5.77 us (3%)
  matrix products  4.92 us (2%)
    all_to_all x1, waiting for transfers between devices, per_device(): lax.all_to_all(field, 'rad', split_axis=2, concat_axis=0, tiled=True)  87.4 us
    all_gather x1, waiting for transfers between devices, per_device(): lax.all_gather(projection, 'rad', axis=0, tiled=True)  35 us
    unnamed x15, local copies, waits for them, and re-layouts  27.2 us
    all_to_all x2, local copies, waits for them, and re-layouts, per_device(): lax.all_to_all(field, 'rad', split_axis=2, concat_axis=0, tiled=True)  12.2 us
    all_to_all x1, starting transfers between devices, per_device(): lax.all_to_all(field, 'rad', split_axis=2, concat_axis=0, tiled=True)  7.47 us
    psum x1, blocking collectives, per_device(): column = lax.psum(local_sum, 'ell')  6.3 us
    pmax x1, blocking collectives, per_device(): top = lax.pmax(local_top, 'ell')  5.96 us
    dot_general x1, matrix products, per_device(): jnp.einsum('rem,ren->emn', exchanged, lax.all_gather(projection, 'rad', a...  4.92 us
  transfers between devices with their start and end apart: 4, of which 3 were waited for; matrix products, arithmetic and copies ran while one was open for 15% of the time, Pallas kernels for 0%

commit v1 on v0

--- a/solution.py
+++ b/solution.py
@@ -5,7 +5,10 @@
 
 
 def per_device(field, projection, ell_ids):
-    exchanged = lax.all_to_all(field, "rad", split_axis=2, concat_axis=0, tiled=True)
+    exchanged = jnp.concatenate(
+        lax.all_to_all(jnp.stack(jnp.split(field, lax.axis_size("rad"), axis=2)), "rad", 0, 0),
+        axis=0,
+    )
     slot_share = exchanged.shape[2]
     coef = jnp.einsum(
         "rem,ren->emn",

time: 219 us -> 226 us (1.032)
  waiting for transfers between devices: 127 us -> 141 us
  local copies, waits for them, and re-layouts: 39.8 us -> 28.6 us
  matrix products: 4.92 us -> 9.64 us
    all_to_all x1, waiting for transfers between devices: 87.4 us -> 100 us  [per_device(): lax.all_to_all(jnp.stack(jnp.split(field, lax.axis_size('rad'), axis=2)),...]
    all_to_all x2 -> x0, local copies, waits for them, and re-layouts: 12.2 us -> none  [per_device(): lax.all_to_all(field, 'rad', split_axis=2, concat_axis=0, tiled=True)]
    dot_general x1, matrix products: 4.92 us -> 9.64 us  [per_device(): jnp.einsum('rem,ren->emn', exchanged, lax.all_gather(projection, 'rad', a...]
    unnamed x15 -> x21, local copies, waits for them, and re-layouts: 27.2 us -> 27.2 us
  transfers between devices with their start and end apart: 4 -> 4, of which waited for: 3 -> 3; matrix products, arithmetic and copies ran while one was open for 15% -> 12% of each run, Pallas kernels for 0% -> 0%
where the time goes in v1:
time: 226 us; the launch traced here: 225 us
  waiting for transfers between devices  141 us (62%)
  local copies, waits for them, and re-layouts  28.6 us (13%)
  between operations  14.2 us (6%)
  starting transfers between devices  14 us (6%)
  blocking collectives  12.2 us (5%)
  matrix products  9.64 us (4%)
  other arithmetic  5.77 us (3%)
    all_to_all x1, waiting for transfers between devices, per_device(): lax.all_to_all(jnp.stack(jnp.split(field, lax.axis_size('rad'), axis=2)),...  100 us
    all_gather x1, waiting for transfers between devices, per_device(): lax.all_gather(projection, 'rad', axis=0, tiled=True)  35.8 us
    unnamed x21, local copies, waits for them, and re-layouts  27.2 us
    dot_general x1, matrix products, per_device(): jnp.einsum('rem,ren->emn', exchanged, lax.all_gather(projection, 'rad', a...  9.64 us
    all_to_all x1, starting transfers between devices, per_device(): lax.all_to_all(jnp.stack(jnp.split(field, lax.axis_size('rad'), axis=2)),...  7.29 us
    psum x1, blocking collectives, per_device(): column = lax.psum(local_sum, 'ell')  6.21 us
    pmax x1, blocking collectives, per_device(): top = lax.pmax(local_top, 'ell')  5.96 us
    all_to_all x1, waiting for transfers between devices, per_device(): lax.all_to_all(peak_part[None], 'rad', split_axis=2, concat_axis=0, tiled...  4.82 us
  transfers between devices with their start and end apart: 4, of which 3 were waited for; matrix products, arithmetic and copies ran while one was open for 12% of the time, Pallas kernels for 0%

profile of v1, /device:TPU:0, one launch (start us, length us, event | category | flops | bytes accessed | tf_op | source)
XLA Modules:
  0.0 225.3 jit_solution(3719334855987009365)
XLA Ops:
  7.2 2.9 %copy.16 = bf16[64,32,256]{2,0,1:T(8,128)(2,1)} copy(bf16[64,32,256]{2,1,0:T(8,128)(2,1)} %param.4) | data formatting | bytes 2097152 | tf_op args[1]
  10.2 1.9 bitcast_dynamic-update-slice_fusion.7
  12.1 1.1 bitcast_dynamic-update-slice_fusion.6
  13.2 0.9 bitcast_dynamic-update-slice_fusion.5
  14.1 1.0 bitcast_dynamic-update-slice_fusion.4
  15.1 0.9 bitcast_dynamic-update-slice_fusion.3
  16.0 1.0 bitcast_dynamic-update-slice_fusion.2
  17.0 0.9 bitcast_dynamic-update-slice_fusion.1
  17.9 1.0 bitcast_dynamic-update-slice_fusion
  19.0 7.7 %reshape.49 = bf16[8,2,65536]{2,1,0:T(2,128)(2,1)} reshape(bf16[8,64,32,64]{3,2,1,0:T(8,128)(2,1)} %bitcast_dynamic-update-slice_fusion) | data formatting | bytes 4194304
  26.7 7.3 %all-to-all-start = ((bf16[8,2,65536]{2,1,0:T(2,128)(2,1)}), bf16[8,2,65536]{2,1,0:T(2,128)(2,1)S(1)}, u32[]{:S(2)}, u32[]{:S(2)}) async-start(bf16[8,2,65536]{2,1,0:T(2,128)(2,1)} %reshape.49), calls=%async_computation | async-start | bytes 4194304 | tf_op jit(solution)/shard_map/all_to_all | solution.py:9
  34.1 100.2 %all-to-all-done = bf16[8,2,65536]{2,1,0:T(2,128)(2,1)S(1)} async-done(((bf16[8,2,65536]{2,1,0:T(2,128)(2,1)}), bf16[8,2,65536]{2,1,0:T(2,128)(2,1)S(1)}, u32[]{:S(2)}, u32[]{:S(2)}) %all-to-all-start) | async-done | bytes 2097184 | tf_op jit(solution)/shard_map/all_to_all | solution.py:9
  134.3 5.0 %reshape.50 = bf16[8,64,32,64]{3,2,1,0:T(8,128)(2,1)} reshape(bf16[8,2,65536]{2,1,0:T(2,128)(2,1)S(1)} %all-to-all-done) | data formatting | bytes 4194304
  139.4 35.8 %all-gather.2.cloned.1.call-done = bf16[512,32,256]{2,0,1:T(8,128)(2,1)} async-done(((bf16[64,32,256]{2,0,1:T(8,128)(2,1)}), bf16[512,32,256]{2,0,1:T(8,128)(2,1)}) %all-gather.2.cloned.1.call-update) | async-done | bytes 8388624 | tf_op jit(solution)/shard_map/all_gather | solution.py:16
  175.2 9.6 %multiply_reduce_fusion = (f32[32,256]{1,0:T(8,128)S(1)}, f32[32,256]{1,0:T(8,128)S(1)}) fusion(f32[32,64]{1,0:T(8,128)S(1)} %compare_convert_fusion, bf16[512,32,256]{2,0,1:T(8,128)(2,1)} %all-gather.2.cloned.1.call-done, bf16[512,32,64]{2,1,0:T(8,128)(2,1)} %bitcast.28), kind=kOutput, calls=%fused_computation.4 | convolution fusion | flops 540000256 | bytes 10559488 | tf_op jit(solution)/shard_map/rem,ren->emn/dot_general | solution.py:13
  185.5 1.0 reduce.18
  187.2 3.3 %all-to-all-start.2 = ((f32[8,1,1024]{2,1,0:T(1,128)}), f32[8,1,1024]{2,1,0:T(1,128)S(1)}, u32[]{:S(2)}, u32[]{:S(2)}) async-start(f32[8,1,1024]{2,1,0:T(1,128)} %reshape.53), calls=%async_computation.2 | async-start | bytes 65536 | tf_op jit(solution)/shard_map/all_to_all | solution.py:25
  190.6 1.0 reduce.16
  192.3 4.8 %all-to-all-done.2 = f32[8,1,1024]{2,1,0:T(1,128)S(1)} async-done(((f32[8,1,1024]{2,1,0:T(1,128)}), f32[8,1,1024]{2,1,0:T(1,128)S(1)}, u32[]{:S(2)}, u32[]{:S(2)}) %all-to-all-start.2) | async-done | bytes 32800 | tf_op jit(solution)/shard_map/all_to_all | solution.py:25
  197.1 3.3 %all-to-all-start.1 = ((f32[8,1,1024]{2,1,0:T(1,128)}), f32[8,1,1024]{2,1,0:T(1,128)S(1)}, u32[]{:S(2)}, u32[]{:S(2)}) async-start(f32[8,1,1024]{2,1,0:T(1,128)} %reshape.51), calls=%async_computation.1 | async-start | bytes 65536 | tf_op jit(solution)/shard_map/all_to_all | solution.py:24
  201.4 1.0 bitcast_reduce_fusion
  202.6 6.0 %pmax.7 = f32[32]{0:T(128)S(1)} all-reduce(f32[32]{0:T(128)S(1)} %reduce_max.38), channel_id=1, replica_groups=mesh['rad'=8,'ell'=4] {'ell'}, use_global_device_ids=true, to_apply=%region_9.10 | all-reduce | flops 32 | bytes 256 | tf_op jit(solution)/shard_map/pmax | solution.py:32
  210.3 1.0 bitcast_reduce_fusion.1
  211.4 6.2 %psum.7 = f32[32]{0:T(128)S(1)} all-reduce(f32[32]{0:T(128)S(1)} %reduce_sum.38), channel_id=1, replica_groups=mesh['rad'=8,'ell'=4] {'ell'}, use_global_device_ids=true, to_apply=%region_4.0 | all-reduce | flops 32 | bytes 256 | tf_op jit(solution)/shard_map/psum | solution.py:31
  (31 shorter events, 5.9 us)
Async XLA Ops:
  7.2 4.9 %copy-start = (bf16[64,32,512]{2,1,0:T(8,128)(2,1)S(1)}, bf16[64,32,512]{2,1,0:T(8,128)(2,1)}, u32[]{:S(2)}) copy-start(bf16[64,32,512]{2,1,0:T(8,128)(2,1)} %param.3) | copy-start | bytes 6291460
  7.2 168.0 %all-gather.2.cloned.1.call-start = ((), (), s32[]{:S(2)}) async-start(), calls=%async_computation.3 | async-start | bytes 9437184 | tf_op jit(solution)/shard_map/all_gather | solution.py:16
  18.9 15.1 %copy-start.1 = (s32[32]{0:T(128)S(1)}, s32[32]{0:T(128)}, u32[]{:S(2)}) copy-start(s32[32]{0:T(128)} %param.5) | copy-start | bytes 388
  26.7 107.6 %all-to-all-start = ((bf16[8,2,65536]{2,1,0:T(2,128)(2,1)}), bf16[8,2,65536]{2,1,0:T(2,128)(2,1)S(1)}, u32[]{:S(2)}, u32[]{:S(2)}) async-start(bf16[8,2,65536]{2,1,0:T(2,128)(2,1)} %reshape.49), calls=%async_computation | async-start | bytes 4194304 | tf_op jit(solution)/shard_map/all_to_all | solution.py:9
  187.2 10.0 %all-to-all-start.2 = ((f32[8,1,1024]{2,1,0:T(1,128)}), f32[8,1,1024]{2,1,0:T(1,128)S(1)}, u32[]{:S(2)}, u32[]{:S(2)}) async-start(f32[8,1,1024]{2,1,0:T(1,128)} %reshape.53), calls=%async_computation.2 | async-start | bytes 65536 | tf_op jit(solution)/shard_map/all_to_all | solution.py:25
  197.1 12.2 %all-to-all-start.1 = ((f32[8,1,1024]{2,1,0:T(1,128)}), f32[8,1,1024]{2,1,0:T(1,128)S(1)}, u32[]{:S(2)}, u32[]{:S(2)}) async-start(f32[8,1,1024]{2,1,0:T(1,128)} %reshape.51), calls=%async_computation.1 | async-start | bytes 65536 | tf_op jit(solution)/shard_map/all_to_all | solution.py:24
Sparse Core Ops, SparseCore 0:
  10.3 164.8 all-gather.1
